TPU v7x, 256 devices: a whole 4x4x8 slice. The times are simulated.
256 devices in a mesh: expert: 32 (over x, z), vocab: 8 (over y, core).
Axes of the slice: x: 4, y: 4, z: 8, core: 2. Of those that a mesh axis runs over, the one named last changes fastest.
Arguments:
- out_grad: bfloat16 [4096, 4096], P('expert', 'vocab'), may hold values from -6 to 6
- residual_stream: bfloat16 [4096, 4096], P('expert', 'vocab'), may hold values from -228 to 228
- norm_gain: float32 [4096], P('vocab'), may hold values from 0.25 to 51
- expert_ids: int32 [4096, 8], P('expert'), may hold values from 0 to 31, all different within a row; in each aligned block of 128 rows (0 to 127, 128 to 255, ...) at most 38 rows name the same one
- gate_scores: float32 [4096, 8], P('expert'), may hold values from 0.05 to 1
- saved_gate: bfloat16 [32, 1216, 1536], P('expert', None, 'vocab'), may hold values from -6 to 6
- saved_up: bfloat16 [32, 1216, 1536], P('expert', None, 'vocab'), may hold values from -6 to 6
- gate_weight: bfloat16 [32, 4096, 1536], P('expert', None, 'vocab'), may hold values from -0.09375 to 0.09375
- up_weight: bfloat16 [32, 4096, 1536], P('expert', None, 'vocab'), may hold values from -0.09375 to 0.09375
- down_weight: bfloat16 [32, 1536, 4096], P('expert', 'vocab'), may hold values from -0.15625 to 0.15625
- embedding: bfloat16 [98304, 4096], P(('expert', 'vocab')), may hold values from -0.09375 to 0.09375
- allowed: int32 [98304], P(('expert', 'vocab')), may hold values 0 or 1
- suffix_start: int32 [32], P('expert'), may hold values from 0 to 108
Outputs:
- token_grad: bfloat16 [4096, 4096], P('expert', 'vocab')
- scores: float32 [640, 98304], P(None, ('expert', 'vocab'))
Inputs may be any that keep to these rules, and one draw needn't show every extreme that they name: `expert_ids`: in each aligned block of 128 rows (one behavior) a row names 8 different experts and no expert is named by more than 38 rows; some expert is named by exactly 38 rows in some blocks.
All inputs are finite; a program needn't handle non-finite values. No bound on the sum of `allowed` on one device may be relied on, other than what follows from the above.
Results may differ from a plain program's by a relative error of at most 0.01.
Values may be sent and summed in bfloat16 or wider, within the bound.
No kernel may reach another device: no remote copies, remote signals or barrier semaphores. Data moves between devices by JAX's collectives and lax.ppermute only.
A program may use at most 128 MiB of HBM per device.

v0:
```python
import jax
import jax.numpy as jnp
from jax import lax
from jax.sharding import PartitionSpec as P

D = 4096
SUFFIX = 20


def sent_to_all(value, axis):
    peers = lax.axis_size(axis)
    return lax.all_to_all(
        jnp.broadcast_to(value[None], (peers, *value.shape)), axis, 0, 0, tiled=True
    )


def taken_together(value, axis):
    everything = sent_to_all(value, axis)
    return jnp.sum(everything, axis=0)


def in_order(parts, dim):
    parts = jnp.moveaxis(parts, 0, dim)
    lengths = parts.shape
    return parts.reshape(*lengths[:dim], lengths[dim] * lengths[dim + 1], *lengths[dim + 2 :])


def collect(value, axis, dim):
    return in_order(sent_to_all(value, axis), dim)


def shards(
    out_grad,
    residual_stream,
    norm_gain,
    expert_ids,
    gate_scores,
    saved_gate,
    saved_up,
    gate_weight,
    up_weight,
    down_weight,
    embedding,
    allowed,
    suffix_start,
):
    n_expert = lax.axis_size("expert")
    seq_len, d_slice = out_grad.shape
    top_k = expert_ids.shape[1]
    slot_count = saved_gate.shape[1]
    capacity = slot_count // n_expert
    contract = (((1,), (1,)), ((), ()))
    chosen = expert_ids.reshape(-1)
    matches = (chosen[:, None] == jnp.arange(n_expert, dtype=jnp.int32)[None, :]).astype(jnp.int32)
    before = jnp.cumsum(matches, axis=0) - matches
    position = jnp.sum(before * matches, axis=1)
    target = chosen * capacity + position
    gate_share = gate_scores / jnp.sum(gate_scores, axis=1, keepdims=True)
    routed = (gate_share[:, :, None] * out_grad.astype(jnp.float32)[:, None, :]).astype(
        jnp.bfloat16
    )
    routed = routed.reshape(seq_len * top_k, d_slice)
    buffer = jnp.zeros((slot_count, d_slice), jnp.bfloat16).at[target].set(routed)
    arrived = lax.all_to_all(buffer, "expert", split_axis=0, concat_axis=0, tiled=True)
    incoming = lax.all_gather(arrived, "vocab", axis=1, tiled=True)
    act_grad = lax.dot_general(
        incoming, down_weight[0], contract, preferred_element_type=jnp.float32
    )
    pre_gate = saved_gate[0].astype(jnp.float32)
    pre_up = saved_up[0].astype(jnp.float32)
    sigmoid_g = jax.nn.sigmoid(pre_gate)
    gate_grad = (act_grad * pre_up * sigmoid_g * (1.0 + pre_gate * (1.0 - sigmoid_g))).astype(
        jnp.bfloat16
    )
    up_grad = (act_grad * pre_gate * sigmoid_g).astype(jnp.bfloat16)
    partial_value = lax.dot_general(
        gate_grad, gate_weight[0], contract, preferred_element_type=jnp.float32
    )
    partial_value = partial_value + lax.dot_general(
        up_grad, up_weight[0], contract, preferred_element_type=jnp.float32
    )
    partial_rounded = partial_value.astype(jnp.bfloat16)
    slot_grad = lax.psum_scatter(partial_rounded, "vocab", scatter_dimension=1, tiled=True).astype(
        jnp.float32
    )
    returned = lax.all_to_all(
        slot_grad.astype(jnp.bfloat16), "expert", split_axis=0, concat_axis=0, tiled=True
    ).astype(slot_grad.dtype)
    moe_grad = jnp.sum(returned[target].reshape(seq_len, top_k, d_slice), axis=1)
    resid = residual_stream.astype(jnp.float32)
    sum_squares = taken_together(jnp.sum(resid * resid, axis=1), "vocab")
    inverse = lax.rsqrt(sum_squares / D + 1e-06)
    normed = resid * inverse[:, None]
    scaled = moe_grad * norm_gain[None, :]
    row_project = taken_together(jnp.sum(scaled * normed, axis=1), "vocab") / D
    token_grad = (
        out_grad.astype(jnp.float32) + inverse[:, None] * (scaled - normed * row_project[:, None])
    ).astype(jnp.bfloat16)
    suffix_grad = lax.dynamic_slice_in_dim(token_grad, suffix_start[0], SUFFIX, 0)
    suffix_grad = collect(suffix_grad, "vocab", 1)
    raw_scores = -lax.dot_general(
        lax.all_gather(suffix_grad, "expert", axis=0, tiled=True),
        embedding,
        contract,
        preferred_element_type=jnp.float32,
    )
    scores = jnp.where(allowed[None, :] > 0, raw_scores, jnp.float32(0.0))
    return (token_grad, scores)


def solution(mesh):
    placed = (
        P("expert", "vocab"),
        P("expert", "vocab"),
        P("vocab"),
        P("expert", None),
        P("expert", None),
        P("expert", None, "vocab"),
        P("expert", None, "vocab"),
        P("expert", None, "vocab"),
        P("expert", None, "vocab"),
        P("expert", "vocab", None),
        P(("expert", "vocab"), None),
        P(("expert", "vocab")),
        P("expert"),
    )
    return jax.shard_map(
        shards,
        mesh=mesh,
        in_specs=placed,
        out_specs=(P("expert", "vocab"), P(None, ("expert", "vocab"))),
        check_vma=False,
    )
```

profile of v0, /device:TPU:8, one launch (start us, length us, event | category | flops | bytes accessed | tf_op | source)
XLA Modules:
  0.0 413.3 jit_solution(6126934621142170420)
XLA Ops:
  9.1 9.0 %reduce-window.6 = s32[32,8,128]{2,1,0:T(8,128)S(1)} reduce-window(s32[32,8,128]{2,1,0:T(8,128)S(1)} %fusion.39, s32[]{:T(128)} %constant.7.clone.1), window={size=1x1x128 pad=0_0x0_0x127_0}, to_apply=%region_2.3 | reduce-window | flops 4161536 | bytes 262148 | tf_op jit(solution)/shard_map/reduce-window
  22.8 6.6 %scatter_custom_fusion = bf16[1216,512]{1,0:T(8,128)(2,1)} fusion(s32[1024]{0:T(1024)S(1)} %bitcast.66, f32[128,512]{1,0:T(8,128)S(1)} %convert_element_type.50, f32[1024]{0:T(1024)S(1)} %mul.97, bf16[]{:T(256)} %constant.5.clone.1), kind=kCustom, calls=%fused_computation.16 | custom fusion | flops 1048576 | bytes 1511426 | tf_op jit(solution)/shard_map/scatter | solution.py:63
  29.4 2.3 all_to_all.26
  31.7 46.4 %all_to_all.38 = bf16[32,38,512]{2,1,0:T(8,128)(2,1)} all-to-all(bf16[32,38,512]{2,1,0:T(8,128)(2,1)} %all_to_all.26), channel_id=1, replica_groups=mesh['expert'=32,'vocab'=8] {'expert'}, dimensions={0} | all-to-all | bytes 2490368 | tf_op jit(solution)/shard_map/all_to_all | solution.py:64
  78.1 2.3 all_to_all.28
  80.4 54.2 %all-gather.4.cloned.1.call-done = bf16[1216,4096]{1,0:T(8,128)(2,1)} async-done(((bf16[1216,512]{1,0:T(8,128)(2,1)}), bf16[1216,4096]{1,0:T(8,128)(2,1)}) %all-gather.4.cloned.1.call-update) | async-done | bytes 9961488 | tf_op jit(solution)/shard_map/all_gather | solution.py:65
  134.6 7.6 %fusion.4 = f32[1216,192]{0,1:T(8,128)S(1)} fusion(bf16[1216,4096]{1,0:T(8,128)(2,1)} %all-gather.4.cloned.1.call-done, bf16[1,192,4096]{2,1,0:T(8,128)(2,1)} %param.22), kind=kOutput, calls=%fused_computation.9 | convolution fusion | flops 1912602624 | bytes 12468224 | tf_op jit(solution)/shard_map/dot_general | solution.py:66
  143.2 8.4 %fusion.2 = f32[1216,4096]{1,0:T(8,128)} fusion(bf16[1,4096,192]{1,2,0:T(8,128)(2,1)S(1)} %copy-done.3, f32[1216,192]{0,1:T(8,128)S(1)} %fusion.4, bf16[1,1216,192]{1,2,0:T(8,128)(2,1)S(1)} %copy-done.5, bf16[1,1216,192]{1,2,0:T(8,128)(2,1)S(1)} %copy-done.2), kind=kOutput, calls=%fused_computation.7 | convolution fusion | flops 1915404288 | bytes 23363584 | tf_op jit(solution)/shard_map/dot_general | solution.py:76
  151.6 14.2 %add_convert_fusion = bf16[1216,4096]{1,0:T(8,128)(2,1)} fusion(f32[1216,4096]{1,0:T(8,128)} %fusion.2, bf16[1,4096,192]{1,2,0:T(8,128)(2,1)} %param.21, f32[1216,192]{0,1:T(8,128)} %copy-done.1, bf16[1,1216,192]{1,2,0:T(8,128)(2,1)} %param.18), kind=kOutput, calls=%fused_computation.2 | convolution fusion | flops 1924198400 | bytes 32858112 | tf_op jit(solution)/shard_map/dot_general | solution.py:79
  167.3 4.5 %all-to-all-start = ((f32[8,1,128]{2,1,0:T(1,128)}), f32[8,1,128]{2,1,0:T(1,128)S(1)}, u32[]{:S(2)}, u32[]{:S(2)}) async-start(f32[8,1,128]{2,1,0:T(1,128)} %broadcast_in_dim.16), calls=%async_computation | async-start | bytes 8192 | tf_op jit(solution)/shard_map/all_to_all | solution.py:12
  171.9 55.1 %reduce-scatter.2.cloned.1.call-done = bf16[1216,512]{1,0:T(8,128)(2,1)} async-done(((bf16[1216,4096]{1,0:T(8,128)(2,1)}), bf16[1216,512]{1,0:T(8,128)(2,1)}) %reduce-scatter.2.cloned.1.call-update) | async-done | bytes 1245200 | tf_op jit(solution)/shard_map/reduce_scatter | solution.py:83
  227.0 2.3 all_to_all.29
  229.3 10.2 %all-to-all-start.2 = ((bf16[32,38,512]{2,1,0:T(8,128)(2,1)}), bf16[32,38,512]{2,1,0:T(8,128)(2,1)}, u32[]{:S(2)}, u32[]{:S(2)}) async-start(bf16[32,38,512]{2,1,0:T(8,128)(2,1)} %all_to_all.29), calls=%async_computation.3 | async-start | bytes 2621440 | tf_op jit(solution)/shard_map/all_to_all | solution.py:86
  239.5 34.5 %all-to-all-done.2 = bf16[32,38,512]{2,1,0:T(8,128)(2,1)} async-done(((bf16[32,38,512]{2,1,0:T(8,128)(2,1)}), bf16[32,38,512]{2,1,0:T(8,128)(2,1)}, u32[]{:S(2)}, u32[]{:S(2)}) %all-to-all-start.2) | async-done | bytes 1245216 | tf_op jit(solution)/shard_map/all_to_all | solution.py:86
  274.0 2.7 reshape.102
  276.7 7.0 %gather_fusion = f32[1024,512]{1,0:T(8,128)} fusion(f32[1216,512]{1,0:T(8,128)} %reshape.102, s32[1024]{0:T(1024)S(1)} %broadcast_clamp_fusion), kind=kCustom, calls=%fused_computation | custom fusion | bytes 4198400 | tf_op jit(solution)/shard_map/gather | solution.py:89
  283.6 2.1 bitcast_reduce_fusion
  286.6 5.1 %all-to-all-start.3 = ((f32[8,1,128]{2,1,0:T(1,128)}), f32[8,1,128]{2,1,0:T(1,128)S(1)}, u32[]{:S(2)}, u32[]{:S(2)}) async-start(f32[8,1,128]{2,1,0:T(1,128)} %broadcast_in_dim.18), calls=%async_computation.4 | async-start | bytes 8192 | tf_op jit(solution)/shard_map/all_to_all | solution.py:12
  292.4 3.1 all-to-all-done.3
  296.6 1.1 fusion.34
  297.8 9.2 %all_to_all.39 = bf16[8,20,512]{2,1,0:T(8,128)(2,1)S(1)} all-to-all(bf16[8,20,512]{2,1,0:T(8,128)(2,1)S(1)} %broadcast_in_dim.20), channel_id=1, replica_groups=mesh['expert'=32,'vocab'=8] {'vocab'}, dimensions={0} | all-to-all | bytes 327680 | tf_op jit(solution)/shard_map/all_to_all | solution.py:12
  307.9 84.7 %all-gather.6.cloned.1.call-done = bf16[32,20,4096]{2,1,0:T(8,128)(2,1)} async-done(((bf16[1,20,4096]{2,1,0:T(8,128)(2,1)}), bf16[32,20,4096]{2,1,0:T(8,128)(2,1)}) %all-gather.6.cloned.1.call-update) | async-done | bytes 5242896 | tf_op jit(solution)/shard_map/all_gather | solution.py:102
  392.6 7.8 %reshape.120 = bf16[640,4096]{1,0:T(8,128)(2,1)} reshape(bf16[32,20,4096]{2,1,0:T(8,128)(2,1)} %all-gather.6.cloned.1.call-done) | data formatting | bytes 10485760
  400.4 6.3 %fusion.6 = f32[640,384]{1,0:T(8,128)} fusion(bf16[640,4096]{1,0:T(8,128)(2,1)} %reshape.120, bf16[384,4096]{1,0:T(8,128)(2,1)S(1)} %copy-done, pred[384]{0:T(512)(128)(4,1)S(1)} %broadcast_compare_fusion), kind=kOutput, calls=%fused_computation.15 | convolution fusion | flops 2013757440 | bytes 9372032 | tf_op jit(solution)/shard_map/dot_general | solution.py:101
  (59 shorter events, 12.1 us)
Async XLA Ops:
  7.2 393.3 %copy-start = (bf16[384,4096]{1,0:T(8,128)(2,1)S(1)}, bf16[384,4096]{1,0:T(8,128)(2,1)}, u32[]{:S(2)}) copy-start(bf16[384,4096]{1,0:T(8,128)(2,1)} %param.23) | copy-start | bytes 9437188
  7.2 127.4 %all-gather.4.cloned.1.call-start = ((), (), s32[]{:S(2)}) async-start(), calls=%async_computation.6 | async-start | bytes 11206656 | tf_op jit(solution)/shard_map/all_gather | solution.py:65
  80.4 146.6 %reduce-scatter.2.cloned.1.call-start = ((), (), s32[]{:S(2)}) async-start(), calls=%async_computation.7 | async-start | bytes 11206656 | tf_op jit(solution)/shard_map/reduce_scatter | solution.py:83
  134.6 8.6 %copy-start.2 = (bf16[1,1216,192]{1,2,0:T(8,128)(2,1)S(1)}, bf16[1,1216,192]{1,2,0:T(8,128)(2,1)}, u32[]{:S(2)}) copy-start(bf16[1,1216,192]{1,2,0:T(8,128)(2,1)} %param.18) | copy-start | bytes 1400836
  134.6 8.6 %copy-start.3 = (bf16[1,4096,192]{1,2,0:T(8,128)(2,1)S(1)}, bf16[1,4096,192]{1,2,0:T(8,128)(2,1)}, u32[]{:S(2)}) copy-start(bf16[1,4096,192]{1,2,0:T(8,128)(2,1)} %param.20) | copy-start | bytes 4718596
  134.6 8.6 %copy-start.5 = (bf16[1,1216,192]{1,2,0:T(8,128)(2,1)S(1)}, bf16[1,1216,192]{1,2,0:T(8,128)(2,1)}, u32[]{:S(2)}) copy-start(bf16[1,1216,192]{1,2,0:T(8,128)(2,1)} %param.19) | copy-start | bytes 1400836
  142.2 0.9 copy-start.1
  165.7 0.9 copy-start.4
  167.3 62.0 %all-to-all-start = ((f32[8,1,128]{2,1,0:T(1,128)}), f32[8,1,128]{2,1,0:T(1,128)S(1)}, u32[]{:S(2)}, u32[]{:S(2)}) async-start(f32[8,1,128]{2,1,0:T(1,128)} %broadcast_in_dim.16), calls=%async_computation | async-start | bytes 8192 | tf_op jit(solution)/shard_map/all_to_all | solution.py:12
  229.3 44.7 %all-to-all-start.2 = ((bf16[32,38,512]{2,1,0:T(8,128)(2,1)}), bf16[32,38,512]{2,1,0:T(8,128)(2,1)}, u32[]{:S(2)}, u32[]{:S(2)}) async-start(bf16[32,38,512]{2,1,0:T(8,128)(2,1)} %all_to_all.29), calls=%async_computation.3 | async-start | bytes 2621440 | tf_op jit(solution)/shard_map/all_to_all | solution.py:86
  283.6 2.1 copy-start.7
  283.6 24.2 %copy-start.8 = (s32[384]{0:T(512)S(1)}, s32[384]{0:T(512)}, u32[]{:S(2)}) copy-start(s32[384]{0:T(512)} %param.24) | copy-start | bytes 4612
  286.6 8.9 %all-to-all-start.3 = ((f32[8,1,128]{2,1,0:T(1,128)}), f32[8,1,128]{2,1,0:T(1,128)S(1)}, u32[]{:S(2)}, u32[]{:S(2)}) async-start(f32[8,1,128]{2,1,0:T(1,128)} %broadcast_in_dim.18), calls=%async_computation.4 | async-start | bytes 8192 | tf_op jit(solution)/shard_map/all_to_all | solution.py:12
  291.7 100.9 %all-gather.6.cloned.1.call-start = ((), (), s32[]{:S(2)}) async-start(), calls=%async_computation.8 | async-start | bytes 6488064 | tf_op jit(solution)/shard_map/all_gather | solution.py:102
  297.7 9.3 %copy-start.6 = (bf16[128,512]{1,0:T(8,128)(2,1)}, bf16[128,512]{1,0:T(8,128)(2,1)S(1)}, u32[]{:S(2)}) copy-start(bf16[128,512]{1,0:T(8,128)(2,1)S(1)} %fusion.34) | copy-start | bytes 393220
Sparse Core Ops, SparseCore 0:
  80.5 54.0 all-gather.3
  165.9 61.0 reduce-scatter.1
  308.0 84.5 all-gather.5
where the time goes:
time: 414 us; the launch traced here: 413 us
  waiting for transfers between devices  232 us (56%)
  blocking collectives  55.6 us (13%)
  matrix products  36.5 us (9%)
  local copies, waits for them, and re-layouts  31.6 us (8%)
  other arithmetic  23.5 us (6%)
  starting transfers between devices  19.9 us (5%)
  between operations  14.6 us (4%)
    all_gather x1, waiting for transfers between devices, shards(): lax.all_gather(suffix_grad, 'expert', axis=0, tiled=True)  84.7 us
    reduce_scatter x1, waiting for transfers between devices, shards(): lax.psum_scatter(partial_rounded, 'vocab', scatter_dimension=1, tiled=True)  55.1 us
    all_gather x1, waiting for transfers between devices, shards(): incoming = lax.all_gather(arrived, 'vocab', axis=1, tiled=True)  54.2 us
    all_to_all x1, blocking collectives, shards(): lax.all_to_all(buffer, 'expert', split_axis=0, concat_axis=0, tiled=True)  46.4 us
    all_to_all x1, waiting for transfers between devices, shards(): lax.all_to_all(slot_grad.astype(jnp.bfloat16), 'expert', split_axis=0, co...  34.5 us
    dot_general x1, matrix products, shards(): lax.dot_general(up_grad, up_weight[0], contract, preferred_element_type=j...  14.2 us
    unnamed x21, local copies, waits for them, and re-layouts  11.4 us
    all_to_all x1, starting transfers between devices, shards(): lax.all_to_all(slot_grad.astype(jnp.bfloat16), 'expert', split_axis=0, co...  10.2 us
  transfers between devices with their start and end apart: 6, of which 5 were waited for; matrix products, arithmetic and copies ran while one was open for 0% of the time, Pallas kernels for 0%

commit v1 on v0

--- a/solution.py
+++ b/solution.py
@@ -98,11 +98,20 @@
     ).astype(jnp.bfloat16)
     suffix_grad = lax.dynamic_slice_in_dim(token_grad, suffix_start[0], SUFFIX, 0)
     suffix_grad = collect(suffix_grad, "vocab", 1)
+
+    def _supply_numbers(field_in):
+        return jnp.concatenate(
+            lax.all_to_all(
+                jnp.stack(tuple((field_in for _ in range(lax.psum(1, "expert")))), axis=0),
+                "expert",
+                split_axis=0,
+                concat_axis=0,
+            ),
+            axis=0,
+        )
+
     raw_scores = -lax.dot_general(
-        lax.all_gather(suffix_grad, "expert", axis=0, tiled=True),
-        embedding,
-        contract,
-        preferred_element_type=jnp.float32,
+        _supply_numbers(suffix_grad), embedding, contract, preferred_element_type=jnp.float32
     )
     scores = jnp.where(allowed[None, :] > 0, raw_scores, jnp.float32(0.0))
     return (token_grad, scores)

time: 414 us -> 479 us (1.16)
  waiting for transfers between devices: 232 us -> 288 us
  starting transfers between devices: 19.9 us -> 26 us
    all_to_all x0 -> x1, waiting for transfers between devices: none -> 141 us  [_supply_numbers(): lax.all_to_all(jnp.stack(tuple((field_in for _ in range(lax.psum(1, 'expe...]
    all_gather x1 -> x0, waiting for transfers between devices: 84.7 us -> none  [shards(): lax.all_gather(suffix_grad, 'expert', axis=0, tiled=True)]
    unnamed x21, local copies, waits for them, and re-layouts: 11.4 us -> 2.87 us
    reshape x0 -> x1, local copies, waits for them, and re-layouts: none -> 7.84 us  [_supply_numbers(): jnp.concatenate(lax.all_to_all(jnp.stack(tuple((field_in for _ in range(l...]
    all_to_all x0 -> x1, starting transfers between devices: none -> 6.05 us  [_supply_numbers(): lax.all_to_all(jnp.stack(tuple((field_in for _ in range(lax.psum(1, 'expe...]
where the time goes in v1:
time: 479 us; the launch traced here: 477 us
  waiting for transfers between devices  288 us (60%)
  blocking collectives  55.6 us (12%)
  matrix products  36.5 us (8%)
  local copies, waits for them, and re-layouts  34.3 us (7%)
  starting transfers between devices  26 us (5%)
  other arithmetic  22.3 us (5%)
  between operations  14.9 us (3%)
    all_to_all x1, waiting for transfers between devices, _supply_numbers(): lax.all_to_all(jnp.stack(tuple((field_in for _ in range(lax.psum(1, 'expe...  141 us
    reduce_scatter x1, waiting for transfers between devices, shards(): lax.psum_scatter(partial_rounded, 'vocab', scatter_dimension=1, tiled=True)  55.1 us
    all_gather x1, waiting for transfers between devices, shards(): incoming = lax.all_gather(arrived, 'vocab', axis=1, tiled=True)  54.2 us
    all_to_all x1, blocking collectives, shards(): lax.all_to_all(buffer, 'expert', split_axis=0, concat_axis=0, tiled=True)  46.4 us
    all_to_all x1, waiting for transfers between devices, shards(): lax.all_to_all(slot_grad.astype(jnp.bfloat16), 'expert', split_axis=0, co...  34.5 us
    dot_general x1, matrix products, shards(): lax.dot_general(up_grad, up_weight[0], contract, preferred_element_type=j...  14.2 us
    all_to_all x1, starting transfers between devices, shards(): lax.all_to_all(slot_grad.astype(jnp.bfloat16), 'expert', split_axis=0, co...  10.2 us
    all_to_all x2, starting transfers between devices, sent_to_all(): lax.all_to_all(jnp.broadcast_to(value[None], (peers, *value.shape)), axis...  9.67 us
  transfers between devices with their start and end apart: 6, of which 5 were waited for; matrix products, arithmetic and copies ran while one was open for 0% of the time, Pallas kernels for 0%

profile of v1, /device:TPU:8, one launch (start us, length us, event | category | flops | bytes accessed | tf_op | source)
XLA Modules:
  0.0 477.1 jit_solution(7408411396727869910)
XLA Ops:
  9.1 9.0 %reduce-window.6 = s32[32,8,128]{2,1,0:T(8,128)S(1)} reduce-window(s32[32,8,128]{2,1,0:T(8,128)S(1)} %fusion.39, s32[]{:T(128)} %constant.7.clone.1), window={size=1x1x128 pad=0_0x0_0x127_0}, to_apply=%region_2.3 | reduce-window | flops 4161536 | bytes 262148 | tf_op jit(solution)/shard_map/reduce-window
  22.8 6.6 %scatter_custom_fusion = bf16[1216,512]{1,0:T(8,128)(2,1)} fusion(s32[1024]{0:T(1024)S(1)} %bitcast.71, f32[128,512]{1,0:T(8,128)S(1)} %convert_element_type.50, f32[1024]{0:T(1024)S(1)} %mul.97, bf16[]{:T(256)} %constant.5.clone.1), kind=kCustom, calls=%fused_computation.16 | custom fusion | flops 1048576 | bytes 1511426 | tf_op jit(solution)/shard_map/scatter | solution.py:63
  29.4 2.3 all_to_all.29
  31.7 46.4 %all_to_all.43 = bf16[32,38,512]{2,1,0:T(8,128)(2,1)} all-to-all(bf16[32,38,512]{2,1,0:T(8,128)(2,1)} %all_to_all.29), channel_id=1, replica_groups=mesh['expert'=32,'vocab'=8] {'expert'}, dimensions={0} | all-to-all | bytes 2490368 | tf_op jit(solution)/shard_map/all_to_all | solution.py:64
  78.1 2.3 all_to_all.31
  80.4 54.2 %all-gather.2.cloned.1.call-done = bf16[1216,4096]{1,0:T(8,128)(2,1)} async-done(((bf16[1216,512]{1,0:T(8,128)(2,1)}), bf16[1216,4096]{1,0:T(8,128)(2,1)}) %all-gather.2.cloned.1.call-update) | async-done | bytes 9961488 | tf_op jit(solution)/shard_map/all_gather | solution.py:65
  134.6 7.6 %fusion.4 = f32[1216,192]{0,1:T(8,128)S(1)} fusion(bf16[1216,4096]{1,0:T(8,128)(2,1)} %all-gather.2.cloned.1.call-done, bf16[1,192,4096]{2,1,0:T(8,128)(2,1)} %param.22), kind=kOutput, calls=%fused_computation.9 | convolution fusion | flops 1912602624 | bytes 12468224 | tf_op jit(solution)/shard_map/dot_general | solution.py:66
  143.2 8.4 %fusion.2 = f32[1216,4096]{1,0:T(8,128)} fusion(bf16[1,4096,192]{1,2,0:T(8,128)(2,1)S(1)} %copy-done.3, f32[1216,192]{0,1:T(8,128)S(1)} %fusion.4, bf16[1,1216,192]{1,2,0:T(8,128)(2,1)S(1)} %copy-done.5, bf16[1,1216,192]{1,2,0:T(8,128)(2,1)S(1)} %copy-done.2), kind=kOutput, calls=%fused_computation.7 | convolution fusion | flops 1915404288 | bytes 23363584 | tf_op jit(solution)/shard_map/dot_general | solution.py:76
  151.6 14.2 %add_convert_fusion = bf16[1216,4096]{1,0:T(8,128)(2,1)} fusion(f32[1216,4096]{1,0:T(8,128)} %fusion.2, bf16[1,4096,192]{1,2,0:T(8,128)(2,1)} %param.21, f32[1216,192]{0,1:T(8,128)} %copy-done.1, bf16[1,1216,192]{1,2,0:T(8,128)(2,1)} %param.18), kind=kOutput, calls=%fused_computation.2 | convolution fusion | flops 1924198400 | bytes 32858112 | tf_op jit(solution)/shard_map/dot_general | solution.py:79
  167.3 4.5 all-to-all-start
  171.9 55.1 %reduce-scatter.2.cloned.1.call-done = bf16[1216,512]{1,0:T(8,128)(2,1)} async-done(((bf16[1216,4096]{1,0:T(8,128)(2,1)}), bf16[1216,512]{1,0:T(8,128)(2,1)}) %reduce-scatter.2.cloned.1.call-update) | async-done | bytes 1245200 | tf_op jit(solution)/shard_map/reduce_scatter | solution.py:83
  227.0 2.3 all_to_all.32
  229.3 10.2 %all-to-all-start.2 = ((bf16[32,38,512]{2,1,0:T(8,128)(2,1)}), bf16[32,38,512]{2,1,0:T(8,128)(2,1)}, u32[]{:S(2)}, u32[]{:S(2)}) async-start(bf16[32,38,512]{2,1,0:T(8,128)(2,1)} %all_to_all.32), calls=%async_computation.3 | async-start | bytes 2621440 | tf_op jit(solution)/shard_map/all_to_all | solution.py:86
  239.5 34.5 %all-to-all-done.2 = bf16[32,38,512]{2,1,0:T(8,128)(2,1)} async-done(((bf16[32,38,512]{2,1,0:T(8,128)(2,1)}), bf16[32,38,512]{2,1,0:T(8,128)(2,1)}, u32[]{:S(2)}, u32[]{:S(2)}) %all-to-all-start.2) | async-done | bytes 1245216 | tf_op jit(solution)/shard_map/all_to_all | solution.py:86
  274.0 2.7 reshape.104
  276.7 7.0 %gather_fusion = f32[1024,512]{1,0:T(8,128)} fusion(f32[1216,512]{1,0:T(8,128)} %reshape.104, s32[1024]{0:T(1024)S(1)} %broadcast_clamp_fusion), kind=kCustom, calls=%fused_computation | custom fusion | bytes 4198400 | tf_op jit(solution)/shard_map/gather | solution.py:89
  286.5 5.1 %all-to-all-start.3 = ((f32[8,1,128]{2,1,0:T(1,128)}), f32[8,1,128]{2,1,0:T(1,128)S(1)}, u32[]{:S(2)}, u32[]{:S(2)}) async-start(f32[8,1,128]{2,1,0:T(1,128)} %broadcast_in_dim.18), calls=%async_computation.4 | async-start | bytes 8192 | tf_op jit(solution)/shard_map/all_to_all | solution.py:12
  292.3 3.1 all-to-all-done.3
  296.6 9.2 %all_to_all.44 = bf16[8,20,512]{2,1,0:T(8,128)(2,1)S(1)} all-to-all(bf16[8,20,512]{2,1,0:T(8,128)(2,1)S(1)} %broadcast_in_dim.20), channel_id=1, replica_groups=mesh['expert'=32,'vocab'=8] {'vocab'}, dimensions={0} | all-to-all | bytes 327680 | tf_op jit(solution)/shard_map/all_to_all | solution.py:12
  306.0 3.4 stack.3
  309.4 6.0 %all-to-all-start.5 = ((bf16[32,20,4096]{2,1,0:T(8,128)(2,1)}), bf16[32,20,4096]{2,1,0:T(8,128)(2,1)}, u32[]{:S(2)}, u32[]{:S(2)}) async-start(bf16[32,20,4096]{2,1,0:T(8,128)(2,1)} %stack.3), calls=%async_computation.6 | async-start | bytes 12582912 | tf_op jit(solution)/shard_map/all_to_all | solution.py:104
  315.5 140.7 %all-to-all-done.5 = bf16[32,20,4096]{2,1,0:T(8,128)(2,1)} async-done(((bf16[32,20,4096]{2,1,0:T(8,128)(2,1)}), bf16[32,20,4096]{2,1,0:T(8,128)(2,1)}, u32[]{:S(2)}, u32[]{:S(2)}) %all-to-all-start.5) | async-done | bytes 5242912 | tf_op jit(solution)/shard_map/all_to_all | solution.py:104
  456.1 7.8 %reshape.101 = bf16[640,4096]{1,0:T(8,128)(2,1)} reshape(bf16[32,20,4096]{2,1,0:T(8,128)(2,1)} %all-to-all-done.5) | data formatting | bytes 10485760 | tf_op jit(solution)/shard_map/reshape | solution.py:103
  464.0 6.3 %fusion.6 = f32[640,384]{1,0:T(8,128)} fusion(bf16[640,4096]{1,0:T(8,128)(2,1)} %reshape.101, bf16[384,4096]{1,0:T(8,128)(2,1)S(1)} %copy-done, pred[384]{0:T(512)(128)(4,1)S(1)} %broadcast_compare_fusion), kind=kOutput, calls=%fused_computation.15 | convolution fusion | flops 2013757440 | bytes 9372032 | tf_op jit(solution)/shard_map/dot_general | solution.py:113
  (60 shorter events, 13.3 us)
Async XLA Ops:
  7.2 456.8 %copy-start = (bf16[384,4096]{1,0:T(8,128)(2,1)S(1)}, bf16[384,4096]{1,0:T(8,128)(2,1)}, u32[]{:S(2)}) copy-start(bf16[384,4096]{1,0:T(8,128)(2,1)} %param.23) | copy-start | bytes 9437188
  7.2 127.4 %all-gather.2.cloned.1.call-start = ((), (), s32[]{:S(2)}) async-start(), calls=%async_computation.7 | async-start | bytes 11206656 | tf_op jit(solution)/shard_map/all_gather | solution.py:65
  80.4 146.6 %reduce-scatter.2.cloned.1.call-start = ((), (), s32[]{:S(2)}) async-start(), calls=%async_computation.8 | async-start | bytes 11206656 | tf_op jit(solution)/shard_map/reduce_scatter | solution.py:83
  134.6 8.6 %copy-start.2 = (bf16[1,1216,192]{1,2,0:T(8,128)(2,1)S(1)}, bf16[1,1216,192]{1,2,0:T(8,128)(2,1)}, u32[]{:S(2)}) copy-start(bf16[1,1216,192]{1,2,0:T(8,128)(2,1)} %param.18) | copy-start | bytes 1400836
  134.6 8.6 %copy-start.3 = (bf16[1,4096,192]{1,2,0:T(8,128)(2,1)S(1)}, bf16[1,4096,192]{1,2,0:T(8,128)(2,1)}, u32[]{:S(2)}) copy-start(bf16[1,4096,192]{1,2,0:T(8,128)(2,1)} %param.20) | copy-start | bytes 4718596
  134.6 8.6 %copy-start.5 = (bf16[1,1216,192]{1,2,0:T(8,128)(2,1)S(1)}, bf16[1,1216,192]{1,2,0:T(8,128)(2,1)}, u32[]{:S(2)}) copy-start(bf16[1,1216,192]{1,2,0:T(8,128)(2,1)} %param.19) | copy-start | bytes 1400836
  142.2 0.9 copy-start.1
  165.7 0.9 copy-start.4
  167.3 62.0 %all-to-all-start = ((f32[8,1,128]{2,1,0:T(1,128)}), f32[8,1,128]{2,1,0:T(1,128)S(1)}, u32[]{:S(2)}, u32[]{:S(2)}) async-start(f32[8,1,128]{2,1,0:T(1,128)} %broadcast_in_dim.16), calls=%async_computation | async-start | bytes 8192 | tf_op jit(solution)/shard_map/all_to_all | solution.py:12
  229.3 44.7 %all-to-all-start.2 = ((bf16[32,38,512]{2,1,0:T(8,128)(2,1)}), bf16[32,38,512]{2,1,0:T(8,128)(2,1)}, u32[]{:S(2)}, u32[]{:S(2)}) async-start(bf16[32,38,512]{2,1,0:T(8,128)(2,1)} %all_to_all.32), calls=%async_computation.3 | async-start | bytes 2621440 | tf_op jit(solution)/shard_map/all_to_all | solution.py:86
  283.6 2.1 copy-start.7
  286.5 8.9 %all-to-all-start.3 = ((f32[8,1,128]{2,1,0:T(1,128)}), f32[8,1,128]{2,1,0:T(1,128)S(1)}, u32[]{:S(2)}, u32[]{:S(2)}) async-start(f32[8,1,128]{2,1,0:T(1,128)} %broadcast_in_dim.18), calls=%async_computation.4 | async-start | bytes 8192 | tf_op jit(solution)/shard_map/all_to_all | solution.py:12
  296.5 9.4 %copy-start.6 = (bf16[128,512]{1,0:T(8,128)(2,1)}, bf16[128,512]{1,0:T(8,128)(2,1)S(1)}, u32[]{:S(2)}) copy-start(bf16[128,512]{1,0:T(8,128)(2,1)S(1)} %fusion.34) | copy-start | bytes 393220
  309.4 6.1 %copy-start.8 = (s32[384]{0:T(512)S(1)}, s32[384]{0:T(512)}, u32[]{:S(2)}) copy-start(s32[384]{0:T(512)} %param.24) | copy-start | bytes 4612
  309.4 146.7 %all-to-all-start.5 = ((bf16[32,20,4096]{2,1,0:T(8,128)(2,1)}), bf16[32,20,4096]{2,1,0:T(8,128)(2,1)}, u32[]{:S(2)}, u32[]{:S(2)}) async-start(bf16[32,20,4096]{2,1,0:T(8,128)(2,1)} %stack.3), calls=%async_computation.6 | async-start | bytes 12582912 | tf_op jit(solution)/shard_map/all_to_all | solution.py:104
Sparse Core Ops, SparseCore 0:
  80.5 54.0 all-gather.1
  165.9 61.0 reduce-scatter.1
